TPU v7x, 256 devices: a whole 4x4x8 slice. The times are simulated.
256 devices in a mesh: ep: 64 (over y, z, core), fs: 4 (over x).
Axes of the slice: x: 4, y: 4, z: 8, core: 2. Of those that a mesh axis runs over, the one named last changes fastest.
Arguments:
- tokens: bfloat16 [8192, 4096], P('ep', 'fs'), may hold values from -6 to 6
- grad_out: bfloat16 [8192, 4096], P('ep', 'fs'), may hold values from -6 to 6
- gate_weight: bfloat16 [4, 14336, 4096], P('fs', 'ep'), may hold values from -0.09375 to 0.09375
- up_weight: bfloat16 [4, 14336, 4096], P('fs', 'ep'), may hold values from -0.09375 to 0.09375
- down_weight: bfloat16 [4, 14336, 4096], P('fs', 'ep'), may hold values from -0.046875 to 0.046875
- gate_values: float32 [4, 256], P('fs'), may hold values from 0.25 to 1
- chosen: int32 [4, 256], replicated, may hold values from 0 to 8191, as said below
- counts: int32 [4], replicated, may hold values from 128 to 256, as said below
Outputs:
- gate_grad: bfloat16 [4, 14336, 4096], P('fs', 'ep')
- up_grad: bfloat16 [4, 14336, 4096], P('fs', 'ep')
- down_grad: bfloat16 [4, 14336, 4096], P('fs', 'ep')
- token_grad: bfloat16 [8192, 4096], P('ep', 'fs')
- score_grad: float32 [4, 256], P('fs')
Inputs may be any that keep to these rules, and one draw needn't show every extreme that they name: `chosen`: the 256 entries of one row are distinct tokens; only the first counts[e] entries of row e are live, the others are padding to be ignored. Among the live entries of one expert at most 6 lie in one aligned block of 128 tokens (the tokens of one index of ep), and in every draw every expert has exactly 6 live entries in some block. `counts`: some expert has all 256 entries live in every draw.
All inputs are finite; a program needn't handle non-finite values.
Results may differ from a plain program's by a relative error of at most 0.0057.
Values may be sent and summed in bfloat16 or wider, within the bound.
No kernel may reach another device: no remote copies, remote signals or barrier semaphores. Data moves between devices by JAX's collectives and lax.ppermute only.
A program may use at most 128 MiB of HBM per device.

v0:
```python
import jax
import jax.numpy as jnp
from jax import lax
from jax.sharding import PartitionSpec as P

SLOTS = 6


def row_products(x_rows, dy_rows, gate_rows, gate_w, up_w, down_w):
    pre_gate = jnp.einsum("rd,hd->rh", x_rows, gate_w, preferred_element_type=jnp.float32)
    pre_up = jnp.einsum("rd,hd->rh", x_rows, up_w, preferred_element_type=jnp.float32)
    sigmoid_val = jax.nn.sigmoid(pre_gate)
    swished = pre_gate * sigmoid_val
    active = (swished * pre_up).astype(jnp.bfloat16)
    probes = jnp.einsum("rd,hd->rh", dy_rows, down_w, preferred_element_type=jnp.float32)
    score_term = jnp.sum(active.astype(jnp.float32) * probes, axis=1)
    weighted = (gate_rows[:, None] * dy_rows.astype(jnp.float32)).astype(jnp.bfloat16)
    d_active = gate_rows[:, None] * probes
    d_gate = (d_active * pre_up * sigmoid_val * (1.0 + pre_gate * (1.0 - sigmoid_val))).astype(
        jnp.bfloat16
    )
    d_up = (d_active * swished).astype(jnp.bfloat16)
    return (active, weighted, d_gate, d_up, score_term)


def weight_grads(stored):
    x_store, weighted_store, active_store, gate_store, up_store = (
        stored[0],
        stored[1],
        stored[2],
        stored[3],
        stored[4],
    )
    grad_g = jnp.einsum("rh,rd->hd", gate_store, x_store, preferred_element_type=jnp.float32)
    grad_u = jnp.einsum("rh,rd->hd", up_store, x_store, preferred_element_type=jnp.float32)
    grad_d = jnp.einsum(
        "rh,rd->hd", active_store, weighted_store, preferred_element_type=jnp.float32
    )
    return (grad_g, grad_u, grad_d)


def input_rows(stored_gate, stored_up, gate_w, up_w):

    def term_rows(row_start, row_count):
        return jnp.dot(stored_gate, gate_w, preferred_element_type=jnp.float32) + jnp.dot(
            stored_up, up_w, preferred_element_type=jnp.float32
        )

    return term_rows


def on_device(tokens, grad_out, gate_weight, up_weight, down_weight, gate_values, chosen, counts):
    ep_count = lax.axis_size("ep")
    ep_index = lax.axis_index("ep")
    fs_index = lax.axis_index("fs")
    tok_rows = tokens.shape[0]
    quarter = tokens.shape[1]
    experts_here = chosen.shape[0]
    total_slots = ep_count * SLOTS
    live = lax.broadcasted_iota(jnp.int32, chosen.shape, 1) < counts[:, None]
    shard_of = chosen // tok_rows
    block_iota = lax.broadcasted_iota(jnp.int32, (1, 1, ep_count), 2)
    one_hot = ((shard_of[:, :, None] == block_iota) & live[:, :, None]).astype(jnp.int32)
    ranks = jnp.sum((jnp.cumsum(one_hot, axis=1) - one_hot) * one_hot, axis=2)
    slot_pos = jnp.where(live, shard_of * SLOTS + ranks, total_slots)
    expert_ids = lax.broadcasted_iota(jnp.int32, chosen.shape, 0)
    slot_token = (
        jnp.full((experts_here, total_slots), -1, jnp.int32)
        .at[expert_ids, slot_pos]
        .set(chosen, mode="drop")
    )
    own_slots = lax.dynamic_slice_in_dim(slot_token, ep_index * SLOTS, SLOTS, 1)
    has_row = own_slots >= 0
    local_rows = jnp.where(has_row, own_slots - ep_index * tok_rows, 0)
    zero_val = jnp.zeros((), tokens.dtype)
    picked_x = jnp.where(has_row[:, :, None], tokens[local_rows], zero_val)
    picked_dy = jnp.where(has_row[:, :, None], grad_out[local_rows], zero_val)
    own_pos = lax.dynamic_index_in_dim(slot_pos, fs_index, 0, keepdims=False)
    own_live = lax.dynamic_index_in_dim(live, fs_index, 0, keepdims=False)
    slot_gate = jnp.zeros((total_slots,), jnp.float32).at[own_pos].set(gate_values[0], mode="drop")
    gate_w = gate_weight[0]
    up_w = up_weight[0]
    down_w = down_weight[0]
    gathered_x, gathered_dy = (
        lax.all_gather(picked_x, "ep", axis=1, tiled=True),
        lax.all_gather(picked_dy, "ep", axis=1, tiled=True),
    )
    whole_x, whole_dy = (
        lax.all_to_all(gathered_x, "fs", split_axis=0, concat_axis=2, tiled=True),
        lax.all_to_all(gathered_dy, "fs", split_axis=0, concat_axis=2, tiled=True),
    )
    x_rows = whole_x[0]
    dy_rows = whole_dy[0]
    active, weighted, d_gate, d_up, score_term = row_products(
        x_rows, dy_rows, slot_gate, gate_w, up_w, down_w
    )
    stored = (x_rows, weighted, active, d_gate, d_up, score_term)
    term_rows = input_rows(stored[3], stored[4], gate_w, up_w)
    partial_rows = term_rows(0, total_slots)
    spread = lax.all_to_all(partial_rows[None], "fs", split_axis=2, concat_axis=0, tiled=True)
    grad_g, grad_u, grad_d = weight_grads(stored)
    returned = lax.psum_scatter(spread, "ep", scatter_dimension=1, tiled=True)
    score_sum = lax.psum(stored[5], "ep")
    safe_pos = jnp.minimum(own_pos, total_slots - 1)
    score_grad = jnp.where(own_live, score_sum[safe_pos], 0.0)[None]
    targets = jnp.where(has_row, local_rows, tok_rows).reshape(-1)
    token_sum = (
        jnp.zeros((tok_rows, quarter), jnp.float32)
        .at[targets]
        .add(returned.reshape(-1, quarter), mode="drop")
    )
    token_grad = token_sum.astype(jnp.bfloat16)
    return (
        grad_g.astype(jnp.bfloat16)[None],
        grad_u.astype(jnp.bfloat16)[None],
        grad_d.astype(jnp.bfloat16)[None],
        token_grad,
        score_grad,
    )


def solution(mesh):
    return jax.shard_map(
        on_device,
        mesh=mesh,
        in_specs=(
            P("ep", "fs"),
            P("ep", "fs"),
            P("fs", "ep", None),
            P("fs", "ep", None),
            P("fs", "ep", None),
            P("fs", None),
            P(),
            P(),
        ),
        out_specs=(
            P("fs", "ep", None),
            P("fs", "ep", None),
            P("fs", "ep", None),
            P("ep", "fs"),
            P("fs", None),
        ),
        check_vma=False,
    )
```

profile of v0, /device:TPU:2, one launch (start us, length us, event | category | flops | bytes accessed | tf_op | source)
XLA Modules:
  0.0 556.3 jit_solution(6767352351725591109)
XLA Ops:
  7.2 0.0 copy-start
  7.2 0.0 all-gather.5.cloned.1.call-start
  7.2 0.8 iota_compare_fusion.2
  8.1 0.7 broadcast_compare_fusion
  8.8 0.7 add_select_fusion
  9.5 0.7 copy.32
  10.3 2.4 reduce-window.6
  12.7 0.1 slice.14
  12.8 0.1 copy.20
  13.0 0.2 fusion.16
  13.1 0.8 fusion.23
  13.9 0.7 and_reduce_fusion
  14.6 0.7 multiply_reduce_fusion.1
  15.4 4.3 scatter_custom_fusion.2
  19.7 0.1 fusion.29
  19.8 0.1 compare_select_fusion.3
  19.9 0.1 reshape.152
  20.0 1.6 gather_fusion.1
  21.6 1.6 gather_fusion
  23.3 0.1 broadcast_select_fusion.1
  23.4 0.7 copy.25
  24.1 0.0 all-gather.5.cloned.1.call-update
  24.1 0.0 all-gather.3.cloned.1.call-start
  24.1 0.7 copy.23
  24.8 0.0 all-gather.3.cloned.1.call-update
  24.8 80.4 %all-gather.5.cloned.1.call-done = bf16[4,384,1024]{2,0,1:T(4,128)(2,1)} async-done(((bf16[4,6,1024]{2,0,1:T(4,128)(2,1)}), bf16[4,384,1024]{2,0,1:T(4,128)(2,1)}) %all-gather.5.cloned.1.call-update) | async-done | bytes 3145744 | tf_op jit(solution)/shard_map/all_gather | solution.py:85
  105.2 6.3 %copy.26 = bf16[4,384,1024]{1,2,0:T(8,128)(2,1)} copy(bf16[4,384,1024]{2,0,1:T(4,128)(2,1)} %all-gather.5.cloned.1.call-done) | data formatting | bytes 6291456 | tf_op jit(solution)/shard_map/all_gather | solution.py:85
  111.5 5.2 all-to-all-start.1
  116.7 67.2 %all-gather.3.cloned.1.call-done = bf16[4,384,1024]{2,0,1:T(4,128)(2,1)} async-done(((bf16[4,6,1024]{2,0,1:T(4,128)(2,1)}), bf16[4,384,1024]{2,0,1:T(4,128)(2,1)}) %all-gather.3.cloned.1.call-update) | async-done | bytes 3145744 | tf_op jit(solution)/shard_map/all_gather | solution.py:86
  184.0 6.3 %copy.24 = bf16[4,384,1024]{1,2,0:T(8,128)(2,1)} copy(bf16[4,384,1024]{2,0,1:T(4,128)(2,1)} %all-gather.3.cloned.1.call-done) | data formatting | bytes 6291456 | tf_op jit(solution)/shard_map/all_gather | solution.py:86
  190.2 0.0 all-to-all-done.1
  190.2 5.2 all-to-all-start
  195.4 0.0 all-reduce.3.cloned.1.call-start
  195.4 1.6 scatter_custom_fusion
  197.0 3.6 fusion.9
  200.5 0.0 copy-done
  200.6 3.0 fusion.6
  203.6 28.7 %all-to-all-done = bf16[4,384,1024]{1,2,0:T(8,128)(2,1)} async-done(((bf16[4,384,1024]{1,2,0:T(8,128)(2,1)}), bf16[4,384,1024]{1,2,0:T(8,128)(2,1)}, u32[]{:S(2)}, u32[]{:S(2)}) %all-to-all-start) | async-done | bytes 3145760 | tf_op jit(solution)/shard_map/all_to_all | solution.py:90
  232.3 3.7 multiply_reduce_fusion
  236.0 0.0 copy-start.2
  236.0 1.0 fusion.4
  237.0 0.5 copy-done.2
  237.5 3.7 add_bitcast_fusion
  241.2 14.8 %copy.27 = f32[1,384,4096]{1,0,2:T(1,128)} copy(f32[1,384,4096]{2,1,0:T(8,128)} %add_bitcast_fusion) | data formatting | bytes 12582912 | tf_op jit(solution)/shard_map/broadcast_in_dim | solution.py:100
  255.9 77.8 %all_to_all.48 = f32[1,384,4096]{1,0,2:T(1,128)} all-to-all(f32[1,384,4096]{1,0,2:T(1,128)} %copy.27), channel_id=1, replica_groups=mesh['ep'=64,'fs'=4] {'fs'}, dimensions={2} | all-to-all | bytes 12582912 | tf_op jit(solution)/shard_map/all_to_all | solution.py:100
  333.7 15.9 %copy.28 = f32[1,384,4,1024]{3,2,1,0:T(4,128)} copy(f32[1,384,4,1024]{1,0,3,2:T(1,128)} %bitcast.91) | data formatting | bytes 12582912 | tf_op jit(solution)/shard_map/all_to_all | solution.py:100
  349.6 0.0 copy-start.3
  349.6 0.0 all-reduce.3.cloned.1.call-update
  349.7 0.1 reshape.144
  349.8 0.6 copy-done.3
  350.3 0.6 dynamic-slice
  351.6 125.2 %psum.7 = f32[384]{0:T(512)S(1)} all-reduce(f32[384]{0:T(512)S(1)} %get-tuple-element.5), channel_id=1, replica_groups=mesh['ep'=64,'fs'=4] {'ep'}, use_global_device_ids=true, to_apply=%region_8.9 | all-reduce | flops 384 | bytes 3072 | tf_op jit(solution)/shard_map/psum | solution.py:103
  476.7 1.9 gather_fusion.2
  478.7 0.6 dynamic-slice_select_fusion
  479.3 4.4 fusion
  483.7 4.4 fusion.1
  488.0 0.0 copy-start.1
  488.0 4.6 fusion.2
  492.6 54.5 %all-reduce.3.cloned.1.call-done = f32[4,384,1024]{2,0,1:T(4,128)} async-done(((f32[4,384,1024]{2,0,1:T(4,128)}), f32[4,384,1024]{2,0,1:T(4,128)}) %all-reduce.3.cloned.1.call-update) | async-done | bytes 6291472
  547.1 0.9 constant_dynamic-slice_fusion.1
  548.0 0.1 copy.29
  548.1 0.9 scatter_custom_fusion.1
  549.0 0.7 convert_element_type.47
  549.7 0.0 copy-done.1
  (17 shorter events, 0.2 us)
Async XLA Ops:
  7.2 193.4 %copy-start = (bf16[1,224,4096]{2,1,0:T(8,128)(2,1)S(1)}, bf16[1,224,4096]{2,1,0:T(8,128)(2,1)}, u32[]{:S(2)}) copy-start(bf16[1,224,4096]{2,1,0:T(8,128)(2,1)} %param.10) | copy-start | bytes 5505028
  7.2 98.0 %all-gather.5.cloned.1.call-start = ((), (), s32[]{:S(2)}) async-start(), calls=%async_computation.4 | async-start | bytes 3194880 | tf_op jit(solution)/shard_map/all_gather | solution.py:85
  24.1 159.9 %all-gather.3.cloned.1.call-start = ((), (), s32[]{:S(2)}) async-start(), calls=%async_computation.3 | async-start | bytes 3194880 | tf_op jit(solution)/shard_map/all_gather | solution.py:86
  111.5 78.7 %all-to-all-start.1 = ((bf16[4,384,1024]{1,2,0:T(8,128)(2,1)}), bf16[4,384,1024]{1,2,0:T(8,128)(2,1)}, u32[]{:S(2)}, u32[]{:S(2)}) async-start(bf16[4,384,1024]{1,2,0:T(8,128)(2,1)} %copy.26), calls=%async_computation.1 | async-start | bytes 6291456 | tf_op jit(solution)/shard_map/all_to_all | solution.py:89
  190.2 42.1 %all-to-all-start = ((bf16[4,384,1024]{1,2,0:T(8,128)(2,1)}), bf16[4,384,1024]{1,2,0:T(8,128)(2,1)}, u32[]{:S(2)}, u32[]{:S(2)}) async-start(bf16[4,384,1024]{1,2,0:T(8,128)(2,1)} %copy.24), calls=%async_computation | async-start | bytes 6291456 | tf_op jit(solution)/shard_map/all_to_all | solution.py:90
  195.4 351.7 %all-reduce.3.cloned.1.call-start = ((), (), s32[]{:S(2)}) async-start(), calls=%async_computation.5 | async-start | bytes 12582912
  236.0 1.5 copy-start.2
  349.6 0.7 copy-start.3
  488.0 61.7 %copy-start.1 = (bf16[1,224,4096]{2,1,0:T(8,128)(2,1)S(1)}, bf16[1,224,4096]{2,1,0:T(8,128)(2,1)}, u32[]{:S(2)}) copy-start(bf16[1,224,4096]{2,1,0:T(8,128)(2,1)} %param.10) | copy-start | bytes 5505028
Sparse Core Ops, SparseCore 0:
  24.2 80.9 all-gather.4
  108.5 75.3 all-gather.2
  349.8 197.2 all-reduce.2
where the time goes:
time: 558 us; the launch traced here: 556 us
  waiting for transfers between devices  231 us (41%)
  blocking collectives  203 us (36%)
  local copies, waits for them, and re-layouts  59.5 us (11%)
  matrix products  28.3 us (5%)
  between operations  14.6 us (3%)
  starting transfers between devices  10.5 us (2%)
  other arithmetic  9.64 us (2%)
    psum x1, blocking collectives, on_device(): score_sum = lax.psum(stored[5], 'ep')  125 us
    all_gather x1, waiting for transfers between devices, on_device(): lax.all_gather(picked_x, 'ep', axis=1, tiled=True)  80.4 us
    all_to_all x1, blocking collectives, on_device(): lax.all_to_all(partial_rows[None], 'fs', split_axis=2, concat_axis=0, til...  77.8 us
    all_gather x1, waiting for transfers between devices, on_device(): lax.all_gather(picked_dy, 'ep', axis=1, tiled=True)  67.2 us
    unnamed x4, waiting for transfers between devices  54.6 us
    all_to_all x1, waiting for transfers between devices, on_device(): lax.all_to_all(gathered_dy, 'fs', split_axis=0, concat_axis=2, tiled=True)  28.7 us
    all_to_all x1, local copies, waits for them, and re-layouts, on_device(): lax.all_to_all(partial_rows[None], 'fs', split_axis=2, concat_axis=0, til...  15.9 us
    broadcast_in_dim x1, local copies, waits for them, and re-layouts, on_device(): partial_rows[None]  14.8 us
  transfers between devices with their start and end apart: 5, of which 4 were waited for; matrix products, arithmetic and copies ran while one was open for 7% of the time, Pallas kernels for 0%

commit v1 on v0

--- a/solution.py
+++ b/solution.py
@@ -4,6 +4,19 @@
 from jax.sharding import PartitionSpec as P
 
 SLOTS = 6
+
+
+def scan_sections(block_here):
+    earlier = jnp.concatenate(
+        lax.all_to_all(
+            jnp.stack(tuple((block_here for _ in range(lax.axis_size("ep"))))),
+            axis_name="ep",
+            split_axis=0,
+            concat_axis=0,
+        ),
+        axis=1,
+    )
+    return earlier
 
 
 def row_products(x_rows, dy_rows, gate_rows, gate_w, up_w, down_w):
@@ -83,7 +96,7 @@
     down_w = down_weight[0]
     gathered_x, gathered_dy = (
         lax.all_gather(picked_x, "ep", axis=1, tiled=True),
-        lax.all_gather(picked_dy, "ep", axis=1, tiled=True),
+        scan_sections(picked_dy),
     )
     whole_x, whole_dy = (
         lax.all_to_all(gathered_x, "fs", split_axis=0, concat_axis=2, tiled=True),

time: 558 us -> 537 us (0.962)
  waiting for transfers between devices: 231 us -> 193 us
  starting transfers between devices: 10.5 us -> 23.6 us
  local copies, waits for them, and re-layouts: 59.5 us -> 65.2 us
    all_gather x1 -> x0, waiting for transfers between devices: 67.2 us -> none  [on_device(): lax.all_gather(picked_dy, 'ep', axis=1, tiled=True)]
    all_to_all x1, waiting for transfers between devices: 0.01 us -> 32.7 us  [on_device(): lax.all_to_all(gathered_x, 'fs', split_axis=0, concat_axis=2, tiled=True)]
    all_to_all x0 -> x1, starting transfers between devices: none -> 12.3 us  [scan_sections(): lax.all_to_all(jnp.stack(tuple((block_here for _ in range(lax.axis_size('...]
    all_gather x1 -> x0, local copies, waits for them, and re-layouts: 6.28 us -> none  [on_device(): lax.all_gather(picked_dy, 'ep', axis=1, tiled=True)]
    unnamed x4 -> x3, waiting for transfers between devices: 54.6 us -> 56.7 us
  transfers between devices with their start and end apart: 5 -> 5, of which waited for: 4 -> 5; matrix products, arithmetic and copies ran while one was open for 7% -> 7% of each run, Pallas kernels for 0% -> 0%
where the time goes in v1:
time: 537 us; the launch traced here: 535 us
  blocking collectives  202 us (38%)
  waiting for transfers between devices  193 us (36%)
  local copies, waits for them, and re-layouts  65.2 us (12%)
  matrix products  26.4 us (5%)
  starting transfers between devices  23.6 us (4%)
  between operations  14.9 us (3%)
  other arithmetic  9.64 us (2%)
    psum x1, blocking collectives, on_device(): score_sum = lax.psum(stored[5], 'ep')  125 us
    all_to_all x1, blocking collectives, on_device(): lax.all_to_all(partial_rows[None], 'fs', split_axis=2, concat_axis=0, til...  77.4 us
    all_gather x1, waiting for transfers between devices, on_device(): lax.all_gather(picked_x, 'ep', axis=1, tiled=True)  74.8 us
    unnamed x3, waiting for transfers between devices  56.7 us
    all_to_all x1, waiting for transfers between devices, on_device(): lax.all_to_all(gathered_x, 'fs', split_axis=0, concat_axis=2, tiled=True)  32.7 us
    all_to_all x1, waiting for transfers between devices, on_device(): lax.all_to_all(gathered_dy, 'fs', split_axis=0, concat_axis=2, tiled=True)  28.1 us
    all_to_all x1, local copies, waits for them, and re-layouts, on_device(): lax.all_to_all(partial_rows[None], 'fs', split_axis=2, concat_axis=0, til...  15.9 us
    broadcast_in_dim x1, local copies, waits for them, and re-layouts, on_device(): partial_rows[None]  14.8 us
  transfers between devices with their start and end apart: 5, of which 5 were waited for; matrix products, arithmetic and copies ran while one was open for 7% of the time, Pallas kernels for 0%

profile of v1, /device:TPU:2, one launch (start us, length us, event | category | flops | bytes accessed | tf_op | source)
XLA Modules:
  0.0 535.0 jit_solution(6158722877677808180)
XLA Ops:
  7.2 0.0 copy-start
  7.2 0.0 all-gather.2.cloned.1.call-start
  7.2 0.8 iota_compare_fusion.2
  8.1 0.7 broadcast_compare_fusion
  8.8 0.7 add_select_fusion
  9.5 0.7 copy.34
  10.3 2.4 reduce-window.6
  12.7 0.1 slice.14
  12.8 0.1 copy.21
  13.0 0.2 fusion.16
  13.1 0.8 fusion.23
  13.9 0.7 and_reduce_fusion
  14.6 0.7 multiply_reduce_fusion.1
  15.4 4.3 scatter_custom_fusion.2
  19.7 0.1 fusion.29
  19.8 0.1 compare_select_fusion.3
  19.9 0.1 reshape.162
  20.0 1.6 gather_fusion.1
  21.6 1.6 gather_fusion
  23.3 0.1 broadcast_select_fusion.1
  23.4 0.7 copy.27
  24.1 0.0 all-gather.2.cloned.1.call-update
  24.1 3.1 stack.2
  27.3 12.3 %all-to-all-start = ((bf16[64,4,6,1024]{3,1,2,0:T(4,128)(2,1)}), bf16[64,4,6,1024]{3,1,2,0:T(4,128)(2,1)}, u32[]{:S(2)}, u32[]{:S(2)}) async-start(bf16[64,4,6,1024]{3,1,2,0:T(4,128)(2,1)} %stack.2), calls=%async_computation | async-start | bytes 6291456 | tf_op jit(solution)/shard_map/all_to_all | solution.py:11
  39.6 74.8 %all-gather.2.cloned.1.call-done = bf16[4,384,1024]{2,0,1:T(4,128)(2,1)} async-done(((bf16[4,6,1024]{2,0,1:T(4,128)(2,1)}), bf16[4,384,1024]{2,0,1:T(4,128)(2,1)}) %all-gather.2.cloned.1.call-update) | async-done | bytes 3145744 | tf_op jit(solution)/shard_map/all_gather | solution.py:98
  114.4 6.3 %copy.28 = bf16[4,384,1024]{1,2,0:T(8,128)(2,1)} copy(bf16[4,384,1024]{2,0,1:T(4,128)(2,1)} %all-gather.2.cloned.1.call-done) | data formatting | bytes 6291456 | tf_op jit(solution)/shard_map/all_gather | solution.py:98
  120.8 0.8 all-to-all-done
  121.6 5.2 all-to-all-start.2
  126.8 4.6 copy.25
  131.3 32.7 %all-to-all-done.2 = bf16[4,384,1024]{1,2,0:T(8,128)(2,1)} async-done(((bf16[4,384,1024]{1,2,0:T(8,128)(2,1)}), bf16[4,384,1024]{1,2,0:T(8,128)(2,1)}, u32[]{:S(2)}, u32[]{:S(2)}) %all-to-all-start.2) | async-done | bytes 3145760 | tf_op jit(solution)/shard_map/all_to_all | solution.py:102
  164.1 6.1 %all-to-all-start.1 = ((bf16[4,384,1024]{2,1,0:T(8,128)(2,1)}), bf16[4,384,1024]{2,1,0:T(8,128)(2,1)}, u32[]{:S(2)}, u32[]{:S(2)}) async-start(bf16[4,384,1024]{2,1,0:T(8,128)(2,1)} %copy.25), calls=%async_computation.1 | async-start | bytes 6291456 | tf_op jit(solution)/shard_map/all_to_all | solution.py:103
  170.1 0.0 all-reduce.3.cloned.1.call-start
  170.1 1.7 scatter_custom_fusion
  171.9 3.6 fusion.9
  175.5 0.0 copy-done
  175.5 3.0 fusion.6
  178.5 28.1 %all-to-all-done.1 = bf16[4,384,1024]{2,1,0:T(8,128)(2,1)} async-done(((bf16[4,384,1024]{2,1,0:T(8,128)(2,1)}), bf16[4,384,1024]{2,1,0:T(8,128)(2,1)}, u32[]{:S(2)}, u32[]{:S(2)}) %all-to-all-start.1) | async-done | bytes 3145760 | tf_op jit(solution)/shard_map/all_to_all | solution.py:103
  206.6 4.7 copy.26
  211.3 3.7 multiply_reduce_fusion
  215.0 0.0 copy-start.3
  215.0 1.0 fusion.4
  216.0 0.5 copy-done.3
  216.5 3.7 add_bitcast_fusion
  220.2 14.8 %copy.29 = f32[1,384,4096]{1,0,2:T(1,128)} copy(f32[1,384,4096]{2,1,0:T(8,128)} %add_bitcast_fusion) | data formatting | bytes 12582912 | tf_op jit(solution)/shard_map/broadcast_in_dim | solution.py:113
  234.9 77.4 %all_to_all.53 = f32[1,384,4096]{1,0,2:T(1,128)} all-to-all(f32[1,384,4096]{1,0,2:T(1,128)} %copy.29), channel_id=1, replica_groups=mesh['ep'=64,'fs'=4] {'fs'}, dimensions={2} | all-to-all | bytes 12582912 | tf_op jit(solution)/shard_map/all_to_all | solution.py:113
  312.3 15.9 %copy.30 = f32[1,384,4,1024]{3,2,1,0:T(4,128)} copy(f32[1,384,4,1024]{1,0,3,2:T(1,128)} %bitcast.94) | data formatting | bytes 12582912 | tf_op jit(solution)/shard_map/all_to_all | solution.py:113
  328.2 0.0 copy-start.4
  328.2 0.0 all-reduce.3.cloned.1.call-update
  328.3 0.1 reshape.154
  328.3 0.6 copy-done.4
  328.9 0.6 dynamic-slice
  330.2 124.7 %psum.7 = f32[384]{0:T(512)S(1)} all-reduce(f32[384]{0:T(512)S(1)} %get-tuple-element.5), channel_id=1, replica_groups=mesh['ep'=64,'fs'=4] {'ep'}, use_global_device_ids=true, to_apply=%region_8.9 | all-reduce | flops 384 | bytes 3072 | tf_op jit(solution)/shard_map/psum | solution.py:116
  454.9 1.9 gather_fusion.2
  456.8 0.6 dynamic-slice_select_fusion
  457.4 4.4 fusion
  461.8 4.5 fusion.1
  466.3 0.0 copy-done.2
  466.3 2.5 fusion.2
  468.9 56.7 %all-reduce.3.cloned.1.call-done = f32[4,384,1024]{2,0,1:T(4,128)} async-done(((f32[4,384,1024]{2,0,1:T(4,128)}), f32[4,384,1024]{2,0,1:T(4,128)}) %all-reduce.3.cloned.1.call-update) | async-done | bytes 6291472
  525.6 0.9 constant_dynamic-slice_fusion.1
  526.5 0.1 copy.31
  526.5 0.9 scatter_custom_fusion.1
  527.5 0.7 convert_element_type.47
  528.2 0.0 copy-done.1
  (20 shorter events, 0.2 us)
Async XLA Ops:
  7.2 168.3 %copy-start = (bf16[1,224,4096]{2,1,0:T(8,128)(2,1)S(1)}, bf16[1,224,4096]{2,1,0:T(8,128)(2,1)}, u32[]{:S(2)}) copy-start(bf16[1,224,4096]{2,1,0:T(8,128)(2,1)} %param.10) | copy-start | bytes 5505028
  7.2 107.3 %all-gather.2.cloned.1.call-start = ((), (), s32[]{:S(2)}) async-start(), calls=%async_computation.4 | async-start | bytes 3194880 | tf_op jit(solution)/shard_map/all_gather | solution.py:98
  27.3 94.3 %all-to-all-start = ((bf16[64,4,6,1024]{3,1,2,0:T(4,128)(2,1)}), bf16[64,4,6,1024]{3,1,2,0:T(4,128)(2,1)}, u32[]{:S(2)}, u32[]{:S(2)}) async-start(bf16[64,4,6,1024]{3,1,2,0:T(4,128)(2,1)} %stack.2), calls=%async_computation | async-start | bytes 6291456 | tf_op jit(solution)/shard_map/all_to_all | solution.py:11
  121.6 42.5 %all-to-all-start.2 = ((bf16[4,384,1024]{1,2,0:T(8,128)(2,1)}), bf16[4,384,1024]{1,2,0:T(8,128)(2,1)}, u32[]{:S(2)}, u32[]{:S(2)}) async-start(bf16[4,384,1024]{1,2,0:T(8,128)(2,1)} %copy.28), calls=%async_computation.2 | async-start | bytes 6291456 | tf_op jit(solution)/shard_map/all_to_all | solution.py:102
  164.1 42.5 %all-to-all-start.1 = ((bf16[4,384,1024]{2,1,0:T(8,128)(2,1)}), bf16[4,384,1024]{2,1,0:T(8,128)(2,1)}, u32[]{:S(2)}, u32[]{:S(2)}) async-start(bf16[4,384,1024]{2,1,0:T(8,128)(2,1)} %copy.25), calls=%async_computation.1 | async-start | bytes 6291456 | tf_op jit(solution)/shard_map/all_to_all | solution.py:103
  170.1 355.4 %all-reduce.3.cloned.1.call-start = ((), (), s32[]{:S(2)}) async-start(), calls=%async_computation.5 | async-start | bytes 12582912
  215.0 1.5 copy-start.3
  328.2 0.7 copy-start.4
  461.8 4.5 copy-start.2
  466.3 61.9 %copy-start.1 = (bf16[1,224,4096]{2,1,0:T(8,128)(2,1)S(1)}, bf16[1,224,4096]{2,1,0:T(8,128)(2,1)}, u32[]{:S(2)}) copy-start(bf16[1,224,4096]{2,1,0:T(8,128)(2,1)} %param.10) | copy-start | bytes 5505028
Sparse Core Ops, SparseCore 0:
  24.2 90.1 all-gather.1
  328.4 197.1 all-reduce.2
